TPU v7x, 1024 devices: a whole 8x8x8 slice. The times are simulated.
1024 devices in a mesh: blk: 16 (over y_hi, x), group: 64 (over z, y_lo, core).
Axes of the slice: x: 8, y: 8 (y_hi: 2, y_lo: 4; y = y_hi * 4 + y_lo), z: 8, core: 2. Of those that a mesh axis runs over, the one named last changes fastest.
Arguments:
- star_pos: float32 [3, 131072], P(None, 'blk'), may hold values from -6 to 6
- star_vel: float32 [3, 131072], P(None, 'blk'), may hold values from -6 to 6
- star_acc: float32 [3, 131072], P(None, 'blk'), may hold values from -6 to 6
- star_jerk: float32 [3, 131072], P(None, 'blk'), may hold values from -6 to 6
- star_mass: float32 [131072], P('blk'), may hold values from 0.25 to 4
- star_dt: float32 [131072], P('blk'), may hold values from 0.0625 to 1
- active_list: int32 [16, 64, 128], P('blk', 'group'), may hold values from 0 to 8191
- active_count: int32 [16, 64], P('blk', 'group'), may hold values from 1 to 128, 2048 in all within a row
Outputs:
- accel_jerk: float32 [16, 64, 6, 128], P('blk', 'group')
Inputs may be any that keep to these rules, and one draw needn't show every extreme that they name: `active_list`: only the first active_count slots of a list are active, the rest are ignored; entries may repeat. `active_count`: for each blk index the counts over group sum to 2048, and one of them is exactly 128.
All inputs are finite; a program needn't handle non-finite values.
Results may differ from a plain program's by a relative error of at most 0.00012.
Values sent between devices are 32-bit elements; how exact they have to be, the bound alone decides.
A program may use at most 32 MiB of HBM per device.

v0:
```python
import jax
import jax.numpy as jnp
from jax import lax
from jax.sharding import PartitionSpec as P

ACT_AVG = 32


soften = 0.01


def predict(pos, vel, acc, jerk, delta):
    step = delta[None, :]
    ppos = pos + step * (vel + step * (0.5 * acc + step * (jerk / 6.0)))
    pvel = vel + step * (acc + step * (0.5 * jerk))
    return (ppos, pvel)


def pair_block(rows, stars):
    gap = stars[0:3, None, :] - rows[0:3, :, None]
    drift = stars[3:6, None, :] - rows[3:6, :, None]
    inverse = lax.rsqrt(jnp.sum(gap * gap, 0) + soften)
    cube = stars[6][None, :] * inverse * inverse * inverse
    radial = 3.0 * jnp.sum(gap * drift, 0) * inverse * inverse
    accel = jnp.sum(gap * cube[None], 2)
    jerks = jnp.sum((drift - radial[None] * gap) * cube[None], 2)
    return jnp.concatenate([accel, jerks], 0)


def pair_sum(rows, stars):
    count = stars.shape[1]
    tile_size = max(128, 262144 // rows.shape[1])

    def advance(total, index):
        piece = lax.dynamic_slice_in_dim(stars, index * tile_size, tile_size, 1)
        return (total + pair_block(rows, piece), None)

    total, _ = lax.scan(
        advance, jnp.zeros((6, rows.shape[1]), jnp.float32), jnp.arange(count // tile_size)
    )
    return total


def compute_forces(rows, stars):
    terms = pair_sum(lax.all_gather(rows, "blk", axis=1, tiled=True), stars)
    return lax.psum_scatter(terms, "blk", scatter_dimension=1, tiled=True)


def on_device(
    star_pos, star_vel, star_acc, star_jerk, star_mass, star_dt, active_list, active_count
):
    ppos, pvel = predict(star_pos, star_vel, star_acc, star_jerk, star_dt)
    total_stars = star_mass.shape[0] * lax.axis_size("blk")
    weight = star_mass / total_stars
    stars = jnp.concatenate([ppos, pvel, weight[None, :]], 0)
    slots = active_list.shape[2]
    rows = jnp.take(jnp.concatenate([ppos, pvel], 0), active_list[0, 0], axis=1)
    mine_count = active_count[0, 0]
    live = jnp.arange(slots, dtype=jnp.int32) < mine_count
    counts = lax.all_gather(active_count, "group", axis=1, tiled=True)[0]
    groups = counts.shape[0]
    capacity = slots // groups
    ends = jnp.cumsum(counts)
    starts = ends - counts
    worker = lax.axis_index("group")
    mine_start = starts[worker]
    peers = jnp.arange(groups, dtype=jnp.int32)[:, None]
    places = jnp.arange(capacity, dtype=jnp.int32)[None, :]
    first = (mine_start - peers + groups - 1) // groups
    offset = peers + groups * (first + places) - mine_start
    valid = offset < mine_count
    picked = jnp.take(rows, jnp.clip(offset, 0, slots - 1).reshape(-1), axis=1).reshape(
        6, groups, capacity
    )
    outgoing = jnp.where(valid[None], picked, jnp.zeros_like(picked))
    arrived = lax.all_to_all(outgoing, "group", split_axis=1, concat_axis=1, tiled=True)
    compact_slot = jnp.arange(ACT_AVG, dtype=jnp.int32)
    position = worker + groups * compact_slot
    owner = jnp.sum((ends[None, :] <= position[:, None]).astype(jnp.int32), 1)
    owner_first = (jnp.take(starts, owner) - worker + groups - 1) // groups
    flat = owner * capacity + (compact_slot - owner_first)
    compact = jnp.take(arrived.reshape(6, groups * capacity), flat, axis=1)
    result = compute_forces(compact, stars)
    back_first = (starts[:, None] - worker + groups - 1) // groups
    back_slot = back_first + places
    back_valid = worker + groups * back_slot < ends[:, None]
    gathered = jnp.take(result, jnp.clip(back_slot, 0, ACT_AVG - 1).reshape(-1), axis=1).reshape(
        6, groups, capacity
    )
    backward = jnp.where(back_valid[None], gathered, jnp.zeros_like(gathered))
    returned = lax.all_to_all(backward, "group", split_axis=1, concat_axis=1, tiled=True)
    row_place = mine_start + jnp.arange(slots, dtype=jnp.int32)
    target = row_place % groups
    slot_of = row_place // groups - (mine_start - target + groups - 1) // groups
    flat_back = target * capacity + jnp.clip(slot_of, 0, capacity - 1)
    forces = jnp.take(returned.reshape(6, groups * capacity), flat_back, axis=1)
    output = jnp.where(live[None, :], forces, jnp.zeros_like(forces))
    return output[None, None]


def solution(mesh):
    return jax.shard_map(
        on_device,
        mesh=mesh,
        in_specs=(
            P(None, "blk"),
            P(None, "blk"),
            P(None, "blk"),
            P(None, "blk"),
            P("blk"),
            P("blk"),
            P("blk", "group", None),
            P("blk", "group"),
        ),
        out_specs=P("blk", "group", None, None),
        check_vma=False,
    )
```

profile of v0, /device:TPU:1, one launch (start us, length us, event | category | flops | bytes accessed | tf_op | source)
XLA Modules:
  0.0 438.3 jit_solution(326135195001726978)
XLA Ops:
  8.5 1.3 dynamic-slice
  10.5 30.5 %all-reduce = s32[64]{0:T(128)S(1)} all-reduce(s32[64]{0:T(128)S(1)} %bitcast_dynamic-update-slice_fusion), channel_id=1, replica_groups=mesh['blk'=16,'group'=64] {'group'}, use_global_device_ids=true, to_apply=%add | all-reduce | flops 64 | bytes 512 | tf_op jit(solution)/shard_map/reshape.271
  43.5 0.8 broadcast_multiply_fusion.2
  44.2 1.2 multiply_add_fusion.1
  45.5 2.6 copy.66
  48.9 2.8 gather_fusion.1
  53.3 8.6 %all-to-all-start = ((f32[6,64,2]{0,2,1:T(2,128)}), f32[6,64,2]{0,2,1:T(2,128)S(1)}, u32[]{:S(2)}, u32[]{:S(2)}) async-start(f32[6,64,2]{0,2,1:T(2,128)} %broadcast_select_fusion), calls=%async_computation | async-start | bytes 131072 | tf_op jit(solution)/shard_map/all_to_all | solution.py:76
  64.0 8.1 %all-to-all-done = f32[6,64,2]{0,2,1:T(2,128)S(1)} async-done(((f32[6,64,2]{0,2,1:T(2,128)}), f32[6,64,2]{0,2,1:T(2,128)S(1)}, u32[]{:S(2)}, u32[]{:S(2)}) %all-to-all-start) | async-done | bytes 3104 | tf_op jit(solution)/shard_map/all_to_all | solution.py:76
  72.8 44.4 %all-gather = f32[16,32,6]{1,2,0:T(8,128)S(1)} all-gather(f32[1,32,6]{1,2,0:T(8,128)S(1)} %copy.67), channel_id=1, replica_groups=mesh['blk'=16,'group'=64] {'blk'}, dimensions={0}, use_global_device_ids=true | all-gather | bytes 13056 | tf_op jit(solution)/shard_map/all_gather | solution.py:45
  117.3 70.2 %while.11 = (s32[]{:T(128)}, f32[6,512]{1,0:T(8,128)S(1)}, s32[16]{0:T(128)S(1)}, f32[7,8192]{1,0:T(8,128)S(1)}, f32[6,512]{1,0:T(8,128)S(1)}, /*index=5*/s32[]{...) while((s32[]{:T(128)}, f32[6,512]{1,0:T(8,128)S(1)}, s32[16]{0:T(128)S(1)}, ...), condition=%wide.region_7.9_spmd.clone, body=%wide.region_2.8_spmd.clone.sunk | while | flops 12326921 | bytes 8542421 | solution.py:38
  118.8 1.0 fusion.20
  120.2 1.5 fusion.21
  123.1 1.0 fusion.20
  124.5 1.5 fusion.21
  127.5 1.0 fusion.20
  128.9 1.5 fusion.21
  131.9 1.0 fusion.20
  133.3 1.5 fusion.21
  136.3 1.0 fusion.20
  137.7 1.5 fusion.21
  140.7 1.0 fusion.20
  142.1 1.5 fusion.21
  145.1 1.0 fusion.20
  146.5 1.5 fusion.21
  149.5 1.0 fusion.20
  150.9 1.5 fusion.21
  153.9 1.0 fusion.20
  155.3 1.5 fusion.21
  158.2 1.0 fusion.20
  159.6 1.5 fusion.21
  162.6 1.0 fusion.20
  164.0 1.5 fusion.21
  167.0 1.0 fusion.20
  168.4 1.5 fusion.21
  171.4 1.0 fusion.20
  172.8 1.5 fusion.21
  175.8 1.0 fusion.20
  177.2 1.5 fusion.21
  180.2 1.0 fusion.20
  181.6 1.5 fusion.21
  184.6 1.0 fusion.20
  186.0 1.5 fusion.21
  187.5 0.8 copy.69
  189.2 213.9 %reduce-scatter.2.cloned.1.call-done = f32[6,32]{0,1:T(8,128)} async-done(((f32[6,512]{0,1:T(8,128)}), f32[6,32]{0,1:T(8,128)}) %reduce-scatter.2.cloned.1.call-update) | async-done | bytes 784 | tf_op jit(solution)/shard_map/reduce_scatter | solution.py:46
  403.1 1.4 gather_fusion.3
  404.5 0.8 select_select_fusion
  405.3 14.7 %all-to-all-start.1 = ((f32[6,64,2]{0,2,1:T(2,128)}), f32[6,64,2]{0,2,1:T(2,128)S(1)}, u32[]{:S(2)}, u32[]{:S(2)}) async-start(f32[6,64,2]{0,2,1:T(2,128)} %select_select_fusion), calls=%async_computation.2 | async-start | bytes 131072 | tf_op jit(solution)/shard_map/all_to_all | solution.py:91
  420.0 10.0 %all-to-all-done.1 = f32[6,64,2]{0,2,1:T(2,128)S(1)} async-done(((f32[6,64,2]{0,2,1:T(2,128)}), f32[6,64,2]{0,2,1:T(2,128)S(1)}, u32[]{:S(2)}, u32[]{:S(2)}) %all-to-all-start.1) | async-done | bytes 3104 | tf_op jit(solution)/shard_map/all_to_all | solution.py:91
  (140 shorter events, 31.0 us)
Async XLA Ops:
  45.5 18.1 %copy-start = (f32[8192]{0:T(1024)S(1)}, f32[8192]{0:T(1024)}, u32[]{:S(2)}) copy-start(f32[8192]{0:T(1024)} %param.16) | copy-start | bytes 98308
  53.3 18.7 %all-to-all-start = ((f32[6,64,2]{0,2,1:T(2,128)}), f32[6,64,2]{0,2,1:T(2,128)S(1)}, u32[]{:S(2)}, u32[]{:S(2)}) async-start(f32[6,64,2]{0,2,1:T(2,128)} %broadcast_select_fusion), calls=%async_computation | async-start | bytes 131072 | tf_op jit(solution)/shard_map/all_to_all | solution.py:76
  61.9 341.2 %reduce-scatter.2.cloned.1.call-start = ((), (), s32[]{:S(2)}) async-start(), calls=%async_computation.3 | async-start | bytes 278528 | tf_op jit(solution)/shard_map/reduce_scatter | solution.py:46
  405.3 24.7 %all-to-all-start.1 = ((f32[6,64,2]{0,2,1:T(2,128)}), f32[6,64,2]{0,2,1:T(2,128)S(1)}, u32[]{:S(2)}, u32[]{:S(2)}) async-start(f32[6,64,2]{0,2,1:T(2,128)} %select_select_fusion), calls=%async_computation.2 | async-start | bytes 131072 | tf_op jit(solution)/shard_map/all_to_all | solution.py:91
Sparse Core Ops, SparseCore 0:
  188.5 214.5 reduce-scatter.1
where the time goes:
time: 439 us; the launch traced here: 438 us
  waiting for transfers between devices  232 us (53%)
  blocking collectives  74.9 us (17%)
  other arithmetic  54.1 us (12%)
  local copies, waits for them, and re-layouts  27.8 us (6%)
  starting transfers between devices  23.3 us (5%)
  between operations  14.3 us (3%)
  loops' own time  11.9 us (3%)
    reduce_scatter x1, waiting for transfers between devices, compute_forces(): return lax.psum_scatter(terms, 'blk', scatter_dimension=1, tiled=True)  214 us
    all_gather x1, blocking collectives, compute_forces(): terms = pair_sum(lax.all_gather(rows, 'blk', axis=1, tiled=True), stars)  44.4 us
    another operation x1, blocking collectives  30.5 us
    reduce_sum x16, other arithmetic, pair_block(): accel = jnp.sum(gap * cube[None], 2)  23.9 us
    reduce_sum x16, other arithmetic, pair_block(): inverse = lax.rsqrt(jnp.sum(gap * gap, 0) + soften)  15.3 us
    all_to_all x1, starting transfers between devices, on_device(): lax.all_to_all(backward, 'group', split_axis=1, concat_axis=1, tiled=True)  14.7 us
    another operation x1, loops' own time, pair_sum(): lax.scan(advance, jnp.zeros((6, rows.shape[1]), jnp.float32), jnp.arange(...  11.9 us
    dynamic_slice x16, local copies, waits for them, and re-layouts, pair_sum(): lax.scan(advance, jnp.zeros((6, rows.shape[1]), jnp.float32), jnp.arange(...  10.7 us
  transfers between devices with their start and end apart: 3, of which 3 were waited for; matrix products, arithmetic and copies ran while one was open for 1% of the time, Pallas kernels for 0%

commit v1 on v0

v1 whole, which is shorter than its diff:
```python
import functools

import jax
import jax.numpy as jnp
from jax import lax
from jax.experimental import pallas as pl
from jax.experimental.pallas import tpu as pltpu
from jax.sharding import PartitionSpec as P

MESH = pl.DeviceIdType.MESH
soften = 0.01
ROWS = 32
LANES = 128
HIGH = lax.Precision.HIGHEST


def pick(index, table):
    value = jnp.int32(table[-1])
    for place in range(len(table) - 2, -1, -1):
        value = jnp.where(index == place, jnp.int32(table[place]), value)
    return value


def chunk_order(high, low):
    def hops(item):
        return 4 * (item[0] % 2) + min(item[1], low - item[1])

    every = sorted([(h, l) for h in range(high) for l in range(low)], key=hops)
    first, rest = every[:3], every[3:]
    return first + rest[::-1]


def kernel(
    dims,
    pos_ref,
    vel_ref,
    acc_ref,
    jerk_ref,
    mass_ref,
    dt_ref,
    list_ref,
    count_ref,
    out_ref,
    tab,
    wide,
    near,
    lists,
    rows,
    res,
    part,
    tiles,
    strip,
    a_send,
    a_recv,
    b_send,
    b_recv,
    r_send,
    r_recv,
    p_send,
    p_recv,
    f_send,
    f_recv,
    g_send,
    g_recv,
):
    n_blk, low, n_far, n_near, total_stars = dims
    high = n_blk // low
    stars = mass_ref.shape[1]
    n_group = n_far * n_near
    order = chunk_order(high, low)
    order_high, order_low = [o[0] for o in order], [o[1] for o in order]
    b = lax.axis_index("blk")
    g = lax.axis_index("group")
    far = g // n_near
    close = lax.rem(g, n_near)

    def far_peer(step):
        return lax.rem(far + step, n_far)

    def near_peer(step):
        return lax.rem(close + step, n_near)

    def blk_peer(place):
        row = lax.rem(b // low + pick(place, order_high), high)
        column = lax.rem(lax.rem(b, low) + pick(place, order_low), low)
        return row * low + column

    barrier = pltpu.get_barrier_semaphore()
    for step in range(1, n_far):
        pl.semaphore_signal(
            barrier, 1, device_id={"group": far_peer(step) * n_near + close}, device_id_type=MESH
        )
    for step in range(1, n_near):
        pl.semaphore_signal(
            barrier, 1, device_id={"group": far * n_near + near_peer(step)}, device_id_type=MESH
        )
    for step in range(1, n_blk):
        pl.semaphore_signal(
            barrier, 1, device_id={"blk": lax.rem(b + step, n_blk)}, device_id_type=MESH
        )

    width = min(1024, stars)

    def predict(index, carry):
        here = pl.ds(pl.multiple_of(index * width, width), width)
        step = dt_ref[:, here]
        vel, acc, jerk = vel_ref[:, here], acc_ref[:, here], jerk_ref[:, here]
        ppos = pos_ref[:, here] + step * (vel + step * (0.5 * acc + step * (jerk / 6.0)))
        pvel = vel + step * (acc + step * (0.5 * jerk))
        weight = mass_ref[:, here] / total_stars
        tab[0:3, here] = ppos
        tab[3:6, here] = pvel
        tab[6:7, here] = weight
        tab[7:8, here] = jnp.zeros_like(weight)
        for row in range(3):
            wide[row, :, here] = jnp.broadcast_to(ppos[row : row + 1], (8, width))
            wide[3 + row, :, here] = jnp.broadcast_to(pvel[row : row + 1], (8, width))
        wide[6, :, here] = jnp.broadcast_to(weight, (8, width))
        return carry

    lax.fori_loop(0, stars // width, predict, 0)

    count = count_ref[0, 0]
    lane = lax.broadcasted_iota(jnp.int32, (1, LANES), 1)
    near[far] = jnp.where(lane < count, list_ref[...], -1)

    pl.semaphore_wait(barrier, (n_far - 1) + (n_near - 1) + (n_blk - 1))

    def a_copy(step, origin):
        return pltpu.make_async_remote_copy(
            src_ref=near.at[origin],
            dst_ref=near.at[origin],
            send_sem=a_send.at[step],
            recv_sem=a_recv.at[step],
            device_id={"group": far_peer(step) * n_near + close},
            device_id_type=MESH,
        )

    def b_copy(step, origin):
        return pltpu.make_async_remote_copy(
            src_ref=near,
            dst_ref=lists.at[origin],
            send_sem=b_send.at[step],
            recv_sem=b_recv.at[step],
            device_id={"group": far * n_near + near_peer(step)},
            device_id_type=MESH,
        )

    for step in range(1, n_far):
        a_copy(step, far).start()
    for step in range(1, n_far):
        a_copy(step, lax.rem(far + n_far - step, n_far)).wait_recv()
    for step in range(1, n_near):
        b_copy(step, close).start()
    lists[close] = near[...]
    for step in range(1, n_near):
        b_copy(step, lax.rem(close + n_near - step, n_near)).wait_recv()

    entry = lists[...].reshape(n_group, LANES)
    valid = entry >= 0
    validf = jnp.where(valid, 1.0, 0.0).astype(jnp.float32)
    entryf = entry.astype(jnp.float32)
    r_iota = lax.broadcasted_iota(jnp.int32, (n_group, n_group), 0)
    c_iota = lax.broadcasted_iota(jnp.int32, (n_group, n_group), 1)
    before = jnp.where(c_iota < r_iota, 1.0, 0.0).astype(jnp.float32)
    starts = jnp.sum(
        jnp.dot(before, validf, preferred_element_type=jnp.float32), axis=1, keepdims=True
    )
    slot = lax.broadcasted_iota(jnp.int32, (n_group, LANES), 1).astype(jnp.float32)
    base = (g * ROWS).astype(jnp.float32)
    place = jnp.where(valid, starts + slot - base, -1.0)
    mine = close * n_far + far
    owner_row = lax.broadcasted_iota(jnp.int32, (n_group, LANES), 0)
    my_start = jnp.sum(
        jnp.sum(jnp.where(owner_row < mine, validf, 0.0), axis=1, keepdims=True),
        axis=0,
        keepdims=True,
    )
    found = jnp.concatenate(
        [
            jnp.sum(jnp.where(place == float(s), entryf, 0.0), axis=0, keepdims=True)
            for s in range(ROWS)
        ],
        axis=0,
    )
    chosen = jnp.sum(found, axis=1, keepdims=True).astype(jnp.int32)
    column = lax.broadcasted_iota(jnp.int32, (ROWS, width), 1)

    def gather(index, total):
        here = pl.ds(pl.multiple_of(index * width, width), width)
        hot = jnp.where(column + index * width == chosen, 1.0, 0.0).astype(jnp.float32)
        return total + lax.dot_general(
            tab[:, here],
            hot,
            (((1,), (1,)), ((), ())),
            precision=HIGH,
            preferred_element_type=jnp.float32,
        )

    picked = lax.fori_loop(0, stars // width, gather, jnp.zeros((8, ROWS), jnp.float32))
    rows[b] = jnp.concatenate([picked, jnp.zeros((8, LANES - ROWS), jnp.float32)], axis=1)

    def r_copy(peer, origin):
        return pltpu.make_async_remote_copy(
            src_ref=rows.at[origin],
            dst_ref=rows.at[origin],
            send_sem=r_send.at[peer],
            recv_sem=r_recv.at[origin],
            device_id={"blk": peer},
            device_id_type=MESH,
        )

    def p_copy(peer, origin):
        return pltpu.make_async_remote_copy(
            src_ref=res.at[peer],
            dst_ref=part.at[origin],
            send_sem=p_send.at[peer],
            recv_sem=p_recv.at[origin],
            device_id={"blk": peer},
            device_id_type=MESH,
        )

    def send_rows(index, carry):
        r_copy(blk_peer(index), b).start()
        return carry

    lax.fori_loop(1, n_blk, send_rows, 0)

    half = 16
    out_lane = lax.broadcasted_iota(jnp.int32, (half, LANES), 1)

    def pairs(index, carry):
        peer = blk_peer(index)

        @pl.when(index > 0)
        def _():
            r_copy(peer, peer).wait_recv()

        across = jnp.transpose(rows[peer])
        pieces = []
        for top in range(0, ROWS, half):
            own = [
                jnp.broadcast_to(across[top : top + half, c : c + 1], (half, LANES))
                for c in range(6)
            ]

            def advance(tile, sums):
                here = pl.ds(pl.multiple_of(tile * LANES, LANES), LANES)
                star = [
                    jnp.concatenate([wide[c, :, here]] * (half // 8), axis=0) for c in range(7)
                ]
                rx, ry, rz = (star[c] - own[c] for c in range(3))
                ux, uy, uz = (star[3 + c] - own[3 + c] for c in range(3))
                inverse = lax.rsqrt((rx * rx + ry * ry) + (rz * rz + soften))
                square = inverse * inverse
                cube = (star[6] * inverse) * square
                radial = (3.0 * square) * (rx * ux + ry * uy + rz * uz)
                return (
                    sums[0] + cube * rx,
                    sums[1] + cube * ry,
                    sums[2] + cube * rz,
                    sums[3] + cube * (ux - radial * rx),
                    sums[4] + cube * (uy - radial * ry),
                    sums[5] + cube * (uz - radial * rz),
                )

            zero = jnp.zeros((half, LANES), jnp.float32)
            sums = lax.fori_loop(0, stars // LANES, advance, (zero,) * 6, unroll=4)
            piece = zero
            for c in range(6):
                piece = jnp.where(out_lane == c, jnp.sum(sums[c], axis=1, keepdims=True), piece)
            pieces.append(piece)
        pieces.append(jnp.zeros((LANES - ROWS, LANES), jnp.float32))
        result = jnp.transpose(jnp.concatenate(pieces, axis=0))[0:8]

        @pl.when(index == 0)
        def _():
            part[b] = result

        @pl.when(index > 0)
        def _():
            res[peer] = result
            p_copy(peer, b).start()

        return carry

    lax.fori_loop(0, n_blk, pairs, 0)

    def take_parts(index, carry):
        peer = blk_peer(index)
        p_copy(peer, peer).wait_recv()
        return carry

    lax.fori_loop(1, n_blk, take_parts, 0)
    force = jnp.sum(part[...], axis=0)

    per_tile = LANES // ROWS
    spread = force
    for turn in range(1, per_tile):
        spread = jnp.where(
            lax.rem(close, per_tile) == turn, pltpu.roll(force, turn * ROWS, 1), spread
        )
    tiles[close] = spread

    def f_copy(step, origin):
        return pltpu.make_async_remote_copy(
            src_ref=tiles.at[origin],
            dst_ref=tiles.at[origin],
            send_sem=f_send.at[step],
            recv_sem=f_recv.at[step],
            device_id={"group": far * n_near + near_peer(step)},
            device_id_type=MESH,
        )

    def g_copy(step, origin):
        return pltpu.make_async_remote_copy(
            src_ref=strip.at[origin],
            dst_ref=strip.at[origin],
            send_sem=g_send.at[step],
            recv_sem=g_recv.at[step],
            device_id={"group": far_peer(step) * n_near + close},
            device_id_type=MESH,
        )

    for step in range(1, n_near):
        f_copy(step, close).start()
    for step in range(1, n_near):
        f_copy(step, lax.rem(close + n_near - step, n_near)).wait_recv()
    n_strip = n_near // per_tile
    for t in range(n_strip):
        joined = tiles[per_tile * t]
        for i in range(1, per_tile):
            joined = joined + tiles[per_tile * t + i]
        strip[far, t] = joined
    for step in range(1, n_far):
        g_copy(step, far).start()
    for step in range(1, n_far):
        g_copy(step, lax.rem(far + n_far - step, n_far)).wait_recv()

    whole = my_start.astype(jnp.int32)
    tile_no, shift = whole // LANES, lax.rem(whole, LANES)
    left = jnp.zeros((8, LANES), jnp.float32)
    right = jnp.zeros((8, LANES), jnp.float32)
    for t in range(n_far * n_strip):
        value = strip[t // n_strip, t % n_strip]
        left = jnp.where(tile_no == t, value, left)
        if t > 0:
            right = jnp.where(tile_no == t - 1, value, right)
    window = jnp.concatenate([left, right], axis=1)
    bit = LANES // 2
    while bit:
        moved = pltpu.roll(window, 2 * LANES - bit, 1)
        window = jnp.where(lax.rem(shift // bit, 2) == 1, moved, window)
        bit //= 2
    out_ref[...] = jnp.where(lane < count, window[0:6, 0:LANES], 0.0)

    for step in range(1, n_far):
        a_copy(step, far).wait_send()
        g_copy(step, far).wait_send()
    for step in range(1, n_near):
        b_copy(step, close).wait_send()
        f_copy(step, close).wait_send()

    def drain(index, carry):
        peer = blk_peer(index)
        r_copy(peer, b).wait_send()
        p_copy(peer, b).wait_send()
        return carry

    lax.fori_loop(1, n_blk, drain, 0)


def on_device(
    low,
    n_near,
    star_pos,
    star_vel,
    star_acc,
    star_jerk,
    star_mass,
    star_dt,
    active_list,
    active_count,
):
    n_blk, n_group = lax.axis_size("blk"), lax.axis_size("group")
    n_far = n_group // n_near
    stars = star_mass.shape[0]
    slots = active_list.shape[2]
    dims = (n_blk, low, n_far, n_near, stars * n_blk)
    vmem = pl.BlockSpec(memory_space=pltpu.VMEM)
    f32, i32 = jnp.float32, jnp.int32
    dma = pltpu.SemaphoreType.DMA
    out = pl.pallas_call(
        functools.partial(kernel, dims),
        out_shape=jax.ShapeDtypeStruct((6, slots), f32),
        in_specs=[vmem] * 7 + [pl.BlockSpec(memory_space=pltpu.SMEM)],
        out_specs=vmem,
        scratch_shapes=[
            pltpu.VMEM((8, stars), f32),
            pltpu.VMEM((7, 8, stars), f32),
            pltpu.VMEM((n_far, 1, LANES), i32),
            pltpu.VMEM((n_near, n_far, 1, LANES), i32),
            pltpu.VMEM((n_blk, 8, LANES), f32),
            pltpu.VMEM((n_blk, 8, LANES), f32),
            pltpu.VMEM((n_blk, 8, LANES), f32),
            pltpu.VMEM((n_near, 8, LANES), f32),
            pltpu.VMEM((n_far, n_near * ROWS // LANES, 8, LANES), f32),
            dma((n_far,)),
            dma((n_far,)),
            dma((n_near,)),
            dma((n_near,)),
            dma((n_blk,)),
            dma((n_blk,)),
            dma((n_blk,)),
            dma((n_blk,)),
            dma((n_near,)),
            dma((n_near,)),
            dma((n_far,)),
            dma((n_far,)),
        ],
        compiler_params=pltpu.CompilerParams(collective_id=0, has_side_effects=True),
    )(
        star_pos,
        star_vel,
        star_acc,
        star_jerk,
        star_mass.reshape(1, stars),
        star_dt.reshape(1, stars),
        active_list.reshape(1, slots),
        active_count,
    )
    return out[None, None]


def solution(mesh):
    n_blk, n_group = mesh.shape["blk"], mesh.shape["group"]
    low = 8 if n_blk % 8 == 0 else n_blk
    n_near = 8 if n_group % 8 == 0 and n_group > 8 else 4
    return jax.shard_map(
        functools.partial(on_device, low, n_near),
        mesh=mesh,
        in_specs=(
            P(None, "blk"),
            P(None, "blk"),
            P(None, "blk"),
            P(None, "blk"),
            P("blk"),
            P("blk"),
            P("blk", "group", None),
            P("blk", "group"),
        ),
        out_specs=P("blk", "group", None, None),
        check_vma=False,
    )
```

time: 439 us -> 86.9 us (0.20)
  waiting for transfers between devices: 232 us -> 0 us
  Pallas kernels: 0 us -> 83.8 us
  blocking collectives: 74.9 us -> 0 us
  other arithmetic: 54.1 us -> 0 us
  local copies, waits for them, and re-layouts: 27.8 us -> 1.26 us
  starting transfers between devices: 23.3 us -> 0 us
  between operations: 14.3 us -> 0.66 us
  loops' own time: 11.9 us -> 0 us
    reduce_scatter x1 -> x0, waiting for transfers between devices: 214 us -> none  [compute_forces(): return lax.psum_scatter(terms, 'blk', scatter_dimension=1, tiled=True)]
    pallas_call x0 -> x1, Pallas kernels: none -> 83.8 us  [on_device(): pl.pallas_call(functools.partial(kernel, dims), out_shape=jax.ShapeDtypeS...]
    all_gather x1 -> x0, blocking collectives: 44.4 us -> none  [compute_forces(): terms = pair_sum(lax.all_gather(rows, 'blk', axis=1, tiled=True), stars)]
    reduce_sum x33 -> x0, other arithmetic: 39.4 us -> none  [the longest x16 23.9 us: pair_block(): accel = jnp.sum(gap * cube[None], 2)]
    another operation x1 -> x0, blocking collectives: 30.5 us -> none
    all_to_all x2 -> x0, starting transfers between devices: 23.3 us -> none  [the longest x1 14.7 us: on_device(): lax.all_to_all(backward, 'group', split_axis=1, concat_axis=1, tiled=True)]
    all_to_all x2 -> x0, waiting for transfers between devices: 18.1 us -> none  [the longest x1 10 us: on_device(): lax.all_to_all(backward, 'group', split_axis=1, concat_axis=1, tiled=True)]
    another operation x1 -> x0, loops' own time: 11.9 us -> none  [pair_sum(): lax.scan(advance, jnp.zeros((6, rows.shape[1]), jnp.float32), jnp.arange(...]
  transfers between devices with their start and end apart: 3 -> 0, of which waited for: 3 -> 0; matrix products, arithmetic and copies ran while one was open for 1% -> 0% of each run, Pallas kernels for 0% -> 0%
where the time goes in v1:
time: 86.9 us; the launch traced here: 85.7 us
  Pallas kernels  83.8 us (96%)
  local copies, waits for them, and re-layouts  1.26 us (1%)
    pallas_call x1, Pallas kernels, on_device(): pl.pallas_call(functools.partial(kernel, dims), out_shape=jax.ShapeDtypeS...  83.8 us

profile of v1, /device:TPU:1, one launch (start us, length us, event | category | flops | bytes accessed | tf_op | source)
XLA Modules:
  0.0 85.7 jit_solution(16787008037644565499)
XLA Ops:
  0.7 83.8 %shard_map.82 = f32[6,128]{1,0:T(8,128)} custom-call(f32[3,8192]{1,0:T(4,128)} %pos_ref.1, f32[3,8192]{1,0:T(4,128)} %vel_ref.1, f32[3,8192]{1,0:T(4,128)} %acc_ref.1, f32[3,8192]{1,0:T(4,128)} %jerk_ref.1, f32[1,8192]{1,0:T(1,128)} %bitcast.4, f32[1,8192]{1,0:T(1,128)} %bitcast.5, s32[1,128]{1,0:T(1,128)} %bitcast.7, s32[1,1]{1,0:T(1,128)S(6)} %copy.10.count_ref), custom_call_target="tpu_custom_call" | custom-call | tf_op jit(solution)/shard_map/pallas_call | solution.py:393
  84.5 1.3 %copy.9 = f32[1,1,6,128]{3,1,2,0:T(1,128)} copy(f32[1,1,6,128]{3,2,1,0:T(8,128)} %bitcast.6) | data formatting | bytes 6144 | tf_op jit(solution)/shard_map/broadcast_in_dim | solution.py:432

commit v2 on v1

--- a/solution.py
+++ b/solution.py
@@ -11,23 +11,18 @@
 soften = 0.01
 ROWS = 32
 LANES = 128
-HIGH = lax.Precision.HIGHEST
-
-
-def pick(index, table):
-    value = jnp.int32(table[-1])
-    for place in range(len(table) - 2, -1, -1):
-        value = jnp.where(index == place, jnp.int32(table[place]), value)
-    return value
-
-
-def chunk_order(high, low):
-    def hops(item):
-        return 4 * (item[0] % 2) + min(item[1], low - item[1])
-
-    every = sorted([(h, l) for h in range(high) for l in range(low)], key=hops)
-    first, rest = every[:3], every[3:]
-    return first + rest[::-1]
+
+
+def split(value):
+    high = value.astype(jnp.bfloat16).astype(jnp.float32)
+    rest = value - high
+    middle = rest.astype(jnp.bfloat16).astype(jnp.float32)
+    return high, middle, (rest - middle).astype(jnp.bfloat16).astype(jnp.float32)
+
+
+def dot(left, right, transposed=False):
+    dims = (((1,), (1 if transposed else 0,)), ((), ()))
+    return lax.dot_general(left, right, dims, preferred_element_type=jnp.float32)
 
 
 def kernel(
@@ -41,7 +36,16 @@
     list_ref,
     count_ref,
     out_ref,
-    tab,
+    pos_in,
+    vel_in,
+    acc_in,
+    jerk_in,
+    mass_in,
+    dt_in,
+    list_in,
+    exact,
+    feature,
+    cross,
     wide,
     near,
     lists,
@@ -62,13 +66,12 @@
     f_recv,
     g_send,
     g_recv,
+    in_sem,
 ):
     n_blk, low, n_far, n_near, total_stars = dims
     high = n_blk // low
     stars = mass_ref.shape[1]
     n_group = n_far * n_near
-    order = chunk_order(high, low)
-    order_high, order_low = [o[0] for o in order], [o[1] for o in order]
     b = lax.axis_index("blk")
     g = lax.axis_index("group")
     far = g // n_near
@@ -81,9 +84,38 @@
         return lax.rem(close + step, n_near)
 
     def blk_peer(place):
-        row = lax.rem(b // low + pick(place, order_high), high)
-        column = lax.rem(lax.rem(b, low) + pick(place, order_low), low)
-        return row * low + column
+        if isinstance(place, int):
+            rank = place
+            if place >= 3:
+                rank = low + 2 - place if place < 3 + low else n_blk + 2 - place
+            turn = (rank + 1) // 2 if rank % 2 else (low - rank // 2) % low
+            rise = 1 if high > 1 and 3 <= place < 3 + low else 0
+        else:
+            rank = jnp.where(place < 3 + low, low + 2 - place, n_blk + 2 - place)
+            rank = jnp.where(place < 3, place, rank)
+            turn = jnp.where(lax.rem(rank, 2) == 1, (rank + 1) // 2, lax.rem(low - rank // 2, low))
+            rise = jnp.int32(0)
+            if high > 1:
+                rise = jnp.where((place >= 3) & (place < 3 + low), 1, 0)
+        row = lax.rem(b // low + rise, high)
+        return row * low + lax.rem(lax.rem(b, low) + turn, low)
+
+    fetch = [
+        pltpu.make_async_copy(source, target, in_sem.at[place])
+        for place, (source, target) in enumerate(
+            [
+                (pos_ref, pos_in),
+                (vel_ref, vel_in),
+                (acc_ref, acc_in),
+                (jerk_ref, jerk_in),
+                (mass_ref, mass_in),
+                (dt_ref, dt_in),
+                (list_ref, list_in),
+            ]
+        )
+    ]
+    for copy in fetch:
+        copy.start()
 
     barrier = pltpu.get_barrier_semaphore()
     for step in range(1, n_far):
@@ -99,30 +131,38 @@
             barrier, 1, device_id={"blk": lax.rem(b + step, n_blk)}, device_id_type=MESH
         )
 
+    for copy in fetch:
+        copy.wait()
+    count = count_ref[0, 0]
+    lane = lax.broadcasted_iota(jnp.int32, (1, LANES), 1)
+    near[far] = jnp.where(lane < count, list_in[...], -1)
+
     width = min(1024, stars)
 
     def predict(index, carry):
         here = pl.ds(pl.multiple_of(index * width, width), width)
-        step = dt_ref[:, here]
-        vel, acc, jerk = vel_ref[:, here], acc_ref[:, here], jerk_ref[:, here]
-        ppos = pos_ref[:, here] + step * (vel + step * (0.5 * acc + step * (jerk / 6.0)))
+        step = dt_in[:, here]
+        vel, acc, jerk = vel_in[:, here], acc_in[:, here], jerk_in[:, here]
+        ppos = pos_in[:, here] + step * (vel + step * (0.5 * acc + step * (jerk / 6.0)))
         pvel = vel + step * (acc + step * (0.5 * jerk))
-        weight = mass_ref[:, here] / total_stars
-        tab[0:3, here] = ppos
-        tab[3:6, here] = pvel
-        tab[6:7, here] = weight
-        tab[7:8, here] = jnp.zeros_like(weight)
+        weight = mass_in[:, here] / total_stars
+        blank = jnp.zeros_like(weight)
         for row in range(3):
             wide[row, :, here] = jnp.broadcast_to(ppos[row : row + 1], (8, width))
-            wide[3 + row, :, here] = jnp.broadcast_to(pvel[row : row + 1], (8, width))
-        wide[6, :, here] = jnp.broadcast_to(weight, (8, width))
+        state = jnp.concatenate([ppos, pvel, blank, blank], axis=0)
+        eight = jnp.zeros_like(state)
+        exact[:, here] = jnp.concatenate([*split(state), eight], axis=0).astype(jnp.bfloat16)
+        scaled = jnp.concatenate([ppos * weight, pvel * weight, weight, blank], axis=0)
+        feature[:, here] = jnp.concatenate([*split(scaled), eight], axis=0).astype(jnp.bfloat16)
+        inner = jnp.sum(ppos * pvel, axis=0, keepdims=True)
+        mixed = jnp.concatenate([ppos, pvel, inner, blank + 1.0], axis=0) * weight
+        big, mid, small = split(mixed)
+        cross[:, here] = jnp.concatenate([big, mid, big, mid, small, big], axis=0).astype(
+            jnp.bfloat16
+        )
         return carry
 
     lax.fori_loop(0, stars // width, predict, 0)
-
-    count = count_ref[0, 0]
-    lane = lax.broadcasted_iota(jnp.int32, (1, LANES), 1)
-    near[far] = jnp.where(lane < count, list_ref[...], -1)
 
     pl.semaphore_wait(barrier, (n_far - 1) + (n_near - 1) + (n_blk - 1))
 
@@ -188,16 +228,13 @@
 
     def gather(index, total):
         here = pl.ds(pl.multiple_of(index * width, width), width)
-        hot = jnp.where(column + index * width == chosen, 1.0, 0.0).astype(jnp.float32)
-        return total + lax.dot_general(
-            tab[:, here],
-            hot,
-            (((1,), (1,)), ((), ())),
-            precision=HIGH,
-            preferred_element_type=jnp.float32,
-        )
-
-    picked = lax.fori_loop(0, stars // width, gather, jnp.zeros((8, ROWS), jnp.float32))
+        hot = jnp.where(column + index * width == chosen, 1.0, 0.0).astype(jnp.bfloat16)
+        return total + dot(exact[:, here], hot, True)
+
+    picked = lax.fori_loop(
+        0, stars // width, gather, jnp.zeros((32, ROWS), jnp.float32), unroll=True
+    )
+    picked = (picked[0:8] + picked[8:16]) + picked[16:24]
     rows[b] = jnp.concatenate([picked, jnp.zeros((8, LANES - ROWS), jnp.float32)], axis=1)
 
     def r_copy(peer, origin):
@@ -220,14 +257,11 @@
             device_id_type=MESH,
         )
 
-    def send_rows(index, carry):
+    for index in range(1, n_blk):
         r_copy(blk_peer(index), b).start()
-        return carry
-
-    lax.fori_loop(1, n_blk, send_rows, 0)
-
-    half = 16
-    out_lane = lax.broadcasted_iota(jnp.int32, (half, LANES), 1)
+
+    span = min(2048, stars)
+    out_lane = lax.broadcasted_iota(jnp.int32, (ROWS, LANES), 1)
 
     def pairs(index, carry):
         peer = blk_peer(index)
@@ -236,42 +270,62 @@
         def _():
             r_copy(peer, peer).wait_recv()
 
-        across = jnp.transpose(rows[peer])
-        pieces = []
-        for top in range(0, ROWS, half):
-            own = [
-                jnp.broadcast_to(across[top : top + half, c : c + 1], (half, LANES))
-                for c in range(6)
-            ]
-
-            def advance(tile, sums):
-                here = pl.ds(pl.multiple_of(tile * LANES, LANES), LANES)
-                star = [
-                    jnp.concatenate([wide[c, :, here]] * (half // 8), axis=0) for c in range(7)
-                ]
-                rx, ry, rz = (star[c] - own[c] for c in range(3))
-                ux, uy, uz = (star[3 + c] - own[3 + c] for c in range(3))
+        own = rows[peer]
+        own_pos, own_vel = own[0:3], own[3:6]
+        inner = jnp.sum(own_pos * own_vel, axis=0, keepdims=True)
+        mixed = jnp.concatenate([-own_vel, -own_pos, jnp.ones_like(inner), inner], axis=0)
+        big, mid, small = split(mixed)
+        fill = jnp.zeros((LANES - 56, LANES), jnp.float32)
+        down = jnp.transpose(
+            jnp.concatenate([big, big, mid, mid, big, small, own, fill], axis=0)
+        )
+        mine_mixed = down[0:ROWS, 0:48].astype(jnp.bfloat16)
+        across = [jnp.broadcast_to(down[0:ROWS, 48 + c : 49 + c], (ROWS, LANES)) for c in range(3)]
+
+        def advance(tile, carried):
+            sums, sx, sy, sz = carried
+            base = pl.multiple_of(tile * span, span)
+            here = pl.ds(base, span)
+            turning = dot(mine_mixed, cross[:, here])
+            tops, rests = [], []
+            for part_at in range(0, span, LANES):
+                at = pl.ds(pl.multiple_of(base + part_at, LANES), LANES)
+                rx, ry, rz = (
+                    jnp.concatenate([wide[c, :, at]] * (ROWS // 8), axis=0) - across[c]
+                    for c in range(3)
+                )
                 inverse = lax.rsqrt((rx * rx + ry * ry) + (rz * rz + soften))
                 square = inverse * inverse
-                cube = (star[6] * inverse) * square
-                radial = (3.0 * square) * (rx * ux + ry * uy + rz * uz)
-                return (
-                    sums[0] + cube * rx,
-                    sums[1] + cube * ry,
-                    sums[2] + cube * rz,
-                    sums[3] + cube * (ux - radial * rx),
-                    sums[4] + cube * (uy - radial * ry),
-                    sums[5] + cube * (uz - radial * rz),
-                )
-
-            zero = jnp.zeros((half, LANES), jnp.float32)
-            sums = lax.fori_loop(0, stars // LANES, advance, (zero,) * 6, unroll=4)
-            piece = zero
-            for c in range(6):
-                piece = jnp.where(out_lane == c, jnp.sum(sums[c], axis=1, keepdims=True), piece)
-            pieces.append(piece)
-        pieces.append(jnp.zeros((LANES - ROWS, LANES), jnp.float32))
-        result = jnp.transpose(jnp.concatenate(pieces, axis=0))[0:8]
+                cube = inverse * square
+                swing = (turning[:, part_at : part_at + LANES] * square) * cube
+                sx, sy, sz = sx + swing * rx, sy + swing * ry, sz + swing * rz
+                top = cube.astype(jnp.bfloat16)
+                tops.append(top)
+                rests.append((cube - top.astype(jnp.float32)).astype(jnp.bfloat16))
+            product = dot(jnp.concatenate(tops, axis=1), feature[:, here], True) + dot(
+                jnp.concatenate(rests, axis=1), feature[:, here], True
+            )
+            return sums + product, sx, sy, sz
+
+        zero = jnp.zeros((ROWS, LANES), jnp.float32)
+        sums, sx, sy, sz = lax.fori_loop(
+            0,
+            stars // span,
+            advance,
+            (jnp.zeros((ROWS, 32), jnp.float32), zero, zero, zero),
+            unroll=True,
+        )
+        piece = jnp.concatenate([sums, jnp.zeros((ROWS, LANES - 32), jnp.float32)], axis=1)
+        for c, total in enumerate((sx, sy, sz)):
+            piece = jnp.where(out_lane == 32 + c, jnp.sum(total, axis=1, keepdims=True), piece)
+        up = jnp.transpose(
+            jnp.concatenate([piece, jnp.zeros((LANES - ROWS, LANES), jnp.float32)], axis=0)
+        )
+        moment = (up[0:8] + up[8:16]) + up[16:24]
+        weighed = moment[6:7]
+        accel = moment[0:3] - own_pos * weighed
+        jerks = (moment[3:6] - own_vel * weighed) - 3.0 * up[32:35]
+        result = jnp.concatenate([accel, jerks, jnp.zeros((2, LANES), jnp.float32)], axis=0)
 
         @pl.when(index == 0)
         def _():
@@ -286,12 +340,9 @@
 
     lax.fori_loop(0, n_blk, pairs, 0)
 
-    def take_parts(index, carry):
+    for index in range(1, n_blk):
         peer = blk_peer(index)
         p_copy(peer, peer).wait_recv()
-        return carry
-
-    lax.fori_loop(1, n_blk, take_parts, 0)
     force = jnp.sum(part[...], axis=0)
 
     per_tile = LANES // ROWS
@@ -352,7 +403,7 @@
         moved = pltpu.roll(window, 2 * LANES - bit, 1)
         window = jnp.where(lax.rem(shift // bit, 2) == 1, moved, window)
         bit //= 2
-    out_ref[...] = jnp.where(lane < count, window[0:6, 0:LANES], 0.0)
+    out_ref[:, 0, :] = jnp.where(lane < count, window[0:6, 0:LANES], 0.0)
 
     for step in range(1, n_far):
         a_copy(step, far).wait_send()
@@ -361,13 +412,10 @@
         b_copy(step, close).wait_send()
         f_copy(step, close).wait_send()
 
-    def drain(index, carry):
+    for index in range(1, n_blk):
         peer = blk_peer(index)
         r_copy(peer, b).wait_send()
         p_copy(peer, b).wait_send()
-        return carry
-
-    lax.fori_loop(1, n_blk, drain, 0)
 
 
 def on_device(
@@ -388,16 +436,22 @@
     slots = active_list.shape[2]
     dims = (n_blk, low, n_far, n_near, stars * n_blk)
     vmem = pl.BlockSpec(memory_space=pltpu.VMEM)
-    f32, i32 = jnp.float32, jnp.int32
+    f32, i32, bf16 = jnp.float32, jnp.int32, jnp.bfloat16
     dma = pltpu.SemaphoreType.DMA
     out = pl.pallas_call(
         functools.partial(kernel, dims),
-        out_shape=jax.ShapeDtypeStruct((6, slots), f32),
-        in_specs=[vmem] * 7 + [pl.BlockSpec(memory_space=pltpu.SMEM)],
+        out_shape=jax.ShapeDtypeStruct((6, 1, slots), f32),
+        in_specs=[pl.BlockSpec(memory_space=pl.ANY)] * 7 + [pl.BlockSpec(memory_space=pltpu.SMEM)],
         out_specs=vmem,
         scratch_shapes=[
-            pltpu.VMEM((8, stars), f32),
-            pltpu.VMEM((7, 8, stars), f32),
+            *[pltpu.VMEM((3, stars), f32)] * 4,
+            pltpu.VMEM((1, stars), f32),
+            pltpu.VMEM((1, stars), f32),
+            pltpu.VMEM((1, slots), i32),
+            pltpu.VMEM((32, stars), bf16),
+            pltpu.VMEM((32, stars), bf16),
+            pltpu.VMEM((48, stars), bf16),
+            pltpu.VMEM((3, 8, stars), f32),
             pltpu.VMEM((n_far, 1, LANES), i32),
             pltpu.VMEM((n_near, n_far, 1, LANES), i32),
             pltpu.VMEM((n_blk, 8, LANES), f32),
@@ -417,6 +471,7 @@
             dma((n_near,)),
             dma((n_far,)),
             dma((n_far,)),
+            dma((7,)),
         ],
         compiler_params=pltpu.CompilerParams(collective_id=0, has_side_effects=True),
     )(
@@ -429,7 +484,7 @@
         active_list.reshape(1, slots),
         active_count,
     )
-    return out[None, None]
+    return out.reshape(1, 1, 6, slots)
 
 
 def solution(mesh):

time: 86.9 us -> 72.2 us (0.83)
  Pallas kernels: 83.8 us -> 69.2 us
    pallas_call x1, Pallas kernels: 83.8 us -> 69.2 us  [on_device(): pl.pallas_call(functools.partial(kernel, dims), out_shape=jax.ShapeDtypeS...]
    broadcast_in_dim x1 -> x0, local copies, waits for them, and re-layouts: 1.26 us -> none  [on_device(): return out[None, None]]
    unnamed x0 -> x1, local copies, waits for them, and re-layouts: none -> 1.26 us
where the time goes in v2:
time: 72.2 us; the launch traced here: 71.1 us
  Pallas kernels  69.2 us (96%)
  local copies, waits for them, and re-layouts  1.26 us (2%)
    pallas_call x1, Pallas kernels, on_device(): pl.pallas_call(functools.partial(kernel, dims), out_shape=jax.ShapeDtypeS...  69.2 us

profile of v2, /device:TPU:1, one launch (start us, length us, event | category | flops | bytes accessed | tf_op | source)
XLA Modules:
  0.0 71.1 jit_solution(10017460914432338803)
XLA Ops:
  0.7 69.2 %shard_map.82 = f32[6,1,128]{2,1,0:T(1,128)} custom-call(f32[3,8192]{1,0:T(4,128)} %pos_ref.1, f32[3,8192]{1,0:T(4,128)} %vel_ref.1, f32[3,8192]{1,0:T(4,128)} %acc_ref.1, f32[3,8192]{1,0:T(4,128)} %jerk_ref.1, f32[1,8192]{1,0:T(1,128)} %bitcast.6, f32[1,8192]{1,0:T(1,128)} %bitcast.7, s32[1,128]{1,0:T(1,128)} %bitcast.9, s32[1,1]{1,0:T(1,128)S(6)} %copy.11.count_ref), custom_call_target="tpu_custom_call" | custom-call | tf_op jit(solution)/shard_map/pallas_call | solution.py:441
  69.9 1.3 %copy.12 = f32[1,1,6,128]{3,1,2,0:T(1,128)} copy(f32[1,1,6,128]{3,1,2,0:T(1,128)} %bitcast.8) | data formatting | bytes 6144

commit v3 on v2

--- a/solution.py
+++ b/solution.py
@@ -83,22 +83,21 @@
     def near_peer(step):
         return lax.rem(close + step, n_near)
 
-    def blk_peer(place):
+    early = max(1, low // 2)
+    row, column = b // low, lax.rem(b, low)
+    other = lax.rem(row + 1, high)
+
+    def peer_at(place):
         if isinstance(place, int):
-            rank = place
-            if place >= 3:
-                rank = low + 2 - place if place < 3 + low else n_blk + 2 - place
+            spot = place if place < early else place - (early if place < early + low else low)
+            rank = spot if spot < 3 else low + 2 - spot
             turn = (rank + 1) // 2 if rank % 2 else (low - rank // 2) % low
-            rise = 1 if high > 1 and 3 <= place < 3 + low else 0
-        else:
-            rank = jnp.where(place < 3 + low, low + 2 - place, n_blk + 2 - place)
-            rank = jnp.where(place < 3, place, rank)
-            turn = jnp.where(lax.rem(rank, 2) == 1, (rank + 1) // 2, lax.rem(low - rank // 2, low))
-            rise = jnp.int32(0)
-            if high > 1:
-                rise = jnp.where((place >= 3) & (place < 3 + low), 1, 0)
-        row = lax.rem(b // low + rise, high)
-        return row * low + lax.rem(lax.rem(b, low) + turn, low)
+            return lax.rem(column + turn, low)
+        spot = jnp.where(place < early + low, place - early, place - low)
+        spot = jnp.where(place < early, place, spot)
+        rank = jnp.where(spot < 3, spot, low + 2 - spot)
+        turn = jnp.where(lax.rem(rank, 2) == 1, (rank + 1) // 2, lax.rem(low - rank // 2, low))
+        return lax.rem(column + turn, low)
 
     fetch = [
         pltpu.make_async_copy(source, target, in_sem.at[place])
@@ -126,10 +125,10 @@
         pl.semaphore_signal(
             barrier, 1, device_id={"group": far * n_near + near_peer(step)}, device_id_type=MESH
         )
-    for step in range(1, n_blk):
-        pl.semaphore_signal(
-            barrier, 1, device_id={"blk": lax.rem(b + step, n_blk)}, device_id_type=MESH
-        )
+    for step in range(1, low):
+        side = row * low + lax.rem(column + step, low)
+        pl.semaphore_signal(barrier, 1, device_id={"blk": side}, device_id_type=MESH)
+    pl.semaphore_signal(barrier, 1, device_id={"blk": other * low + column}, device_id_type=MESH)
 
     for copy in fetch:
         copy.wait()
@@ -164,7 +163,7 @@
 
     lax.fori_loop(0, stars // width, predict, 0)
 
-    pl.semaphore_wait(barrier, (n_far - 1) + (n_near - 1) + (n_blk - 1))
+    pl.semaphore_wait(barrier, (n_far - 1) + (n_near - 1) + low)
 
     def a_copy(step, origin):
         return pltpu.make_async_remote_copy(
@@ -224,11 +223,11 @@
         axis=0,
     )
     chosen = jnp.sum(found, axis=1, keepdims=True).astype(jnp.int32)
-    column = lax.broadcasted_iota(jnp.int32, (ROWS, width), 1)
+    star_no = lax.broadcasted_iota(jnp.int32, (ROWS, width), 1)
 
     def gather(index, total):
         here = pl.ds(pl.multiple_of(index * width, width), width)
-        hot = jnp.where(column + index * width == chosen, 1.0, 0.0).astype(jnp.bfloat16)
+        hot = jnp.where(star_no + index * width == chosen, 1.0, 0.0).astype(jnp.bfloat16)
         return total + dot(exact[:, here], hot, True)
 
     picked = lax.fori_loop(
@@ -237,38 +236,69 @@
     picked = (picked[0:8] + picked[8:16]) + picked[16:24]
     rows[b] = jnp.concatenate([picked, jnp.zeros((8, LANES - ROWS), jnp.float32)], axis=1)
 
-    def r_copy(peer, origin):
+    def r_copy(peer, origin, mark):
         return pltpu.make_async_remote_copy(
             src_ref=rows.at[origin],
             dst_ref=rows.at[origin],
-            send_sem=r_send.at[peer],
+            send_sem=r_send.at[mark],
             recv_sem=r_recv.at[origin],
             device_id={"blk": peer},
             device_id_type=MESH,
         )
 
-    def p_copy(peer, origin):
+    def p_copy(peer, source, slot):
         return pltpu.make_async_remote_copy(
-            src_ref=res.at[peer],
-            dst_ref=part.at[origin],
-            send_sem=p_send.at[peer],
-            recv_sem=p_recv.at[origin],
+            src_ref=res.at[source],
+            dst_ref=part.at[slot],
+            send_sem=p_send.at[source],
+            recv_sem=p_recv.at[slot],
             device_id={"blk": peer},
             device_id_type=MESH,
         )
 
-    for index in range(1, n_blk):
-        r_copy(blk_peer(index), b).start()
+    partner = other * low + column
+    sum_copy = pltpu.make_async_remote_copy(
+        src_ref=res.at[partner],
+        dst_ref=part.at[n_blk],
+        send_sem=p_send.at[partner],
+        recv_sem=p_recv.at[n_blk],
+        device_id={"blk": partner},
+        device_id_type=MESH,
+    )
+
+    def side(step):
+        return lax.rem(column + step, low)
+
+    r_copy(partner, b, partner).start()
+    for place in list(range(1, early)) + list(range(early + low, n_blk)):
+        peer = row * low + peer_at(place)
+        r_copy(peer, b, peer).start()
 
     span = min(2048, stars)
     out_lane = lax.broadcasted_iota(jnp.int32, (ROWS, LANES), 1)
 
     def pairs(index, carry):
-        peer = blk_peer(index)
-
-        @pl.when(index > 0)
+        line = peer_at(index)
+        away = (index >= early) & (index < early + low)
+        peer = jnp.where(away, other, row) * low + line
+
+        @pl.when(index == min(3, early))
         def _():
-            r_copy(peer, peer).wait_recv()
+            r_copy(partner, partner, partner).wait_recv()
+            for step in range(1, low):
+                r_copy(row * low + side(step), partner, other * low + side(step)).start()
+
+        @pl.when((index > 0) & (index != early))
+        def _():
+            r_copy(peer, peer, peer).wait_recv()
+
+        @pl.when(index == n_blk - 1)
+        def _():
+            for step in range(1, low):
+                slot = other * low + side(low - step)
+                p_copy(b, slot, slot).wait_recv()
+            res[partner] = jnp.sum(part[pl.ds(other * low, low)], axis=0)
+            sum_copy.start()
 
         own = rows[peer]
         own_pos, own_vel = own[0:3], own[3:6]
@@ -331,19 +361,24 @@
         def _():
             part[b] = result
 
-        @pl.when(index > 0)
+        @pl.when(index == early)
+        def _():
+            part[partner] = result
+
+        @pl.when((index > 0) & (index != early))
         def _():
             res[peer] = result
-            p_copy(peer, b).start()
+            p_copy(row * low + line, peer, jnp.where(away, other, row) * low + column).start()
 
         return carry
 
     lax.fori_loop(0, n_blk, pairs, 0)
 
-    for index in range(1, n_blk):
-        peer = blk_peer(index)
-        p_copy(peer, peer).wait_recv()
-    force = jnp.sum(part[...], axis=0)
+    for step in range(1, low):
+        slot = row * low + side(low - step)
+        p_copy(b, slot, slot).wait_recv()
+    sum_copy.wait_recv()
+    force = jnp.sum(part[pl.ds(row * low, low)], axis=0) + part[n_blk]
 
     per_tile = LANES // ROWS
     spread = force
@@ -385,6 +420,19 @@
         strip[far, t] = joined
     for step in range(1, n_far):
         g_copy(step, far).start()
+    for step in range(1, n_far):
+        a_copy(step, far).wait_send()
+    for step in range(1, n_near):
+        b_copy(step, close).wait_send()
+        f_copy(step, close).wait_send()
+    r_copy(partner, b, partner).wait_send()
+    sum_copy.wait_send()
+    for step in range(1, low):
+        near_mark, far_mark = row * low + side(step), other * low + side(step)
+        r_copy(near_mark, b, near_mark).wait_send()
+        r_copy(near_mark, partner, far_mark).wait_send()
+        p_copy(near_mark, near_mark, b).wait_send()
+        p_copy(near_mark, far_mark, partner).wait_send()
     for step in range(1, n_far):
         g_copy(step, lax.rem(far + n_far - step, n_far)).wait_recv()
 
@@ -406,16 +454,7 @@
     out_ref[:, 0, :] = jnp.where(lane < count, window[0:6, 0:LANES], 0.0)
 
     for step in range(1, n_far):
-        a_copy(step, far).wait_send()
         g_copy(step, far).wait_send()
-    for step in range(1, n_near):
-        b_copy(step, close).wait_send()
-        f_copy(step, close).wait_send()
-
-    for index in range(1, n_blk):
-        peer = blk_peer(index)
-        r_copy(peer, b).wait_send()
-        p_copy(peer, b).wait_send()
 
 
 def on_device(
@@ -456,7 +495,7 @@
             pltpu.VMEM((n_near, n_far, 1, LANES), i32),
             pltpu.VMEM((n_blk, 8, LANES), f32),
             pltpu.VMEM((n_blk, 8, LANES), f32),
-            pltpu.VMEM((n_blk, 8, LANES), f32),
+            pltpu.VMEM((n_blk + 1, 8, LANES), f32),
             pltpu.VMEM((n_near, 8, LANES), f32),
             pltpu.VMEM((n_far, n_near * ROWS // LANES, 8, LANES), f32),
             dma((n_far,)),
@@ -466,7 +505,7 @@
             dma((n_blk,)),
             dma((n_blk,)),
             dma((n_blk,)),
-            dma((n_blk,)),
+            dma((n_blk + 1,)),
             dma((n_near,)),
             dma((n_near,)),
             dma((n_far,)),
@@ -489,7 +528,7 @@
 
 def solution(mesh):
     n_blk, n_group = mesh.shape["blk"], mesh.shape["group"]
-    low = 8 if n_blk % 8 == 0 else n_blk
+    low = n_blk // 2
     n_near = 8 if n_group % 8 == 0 and n_group > 8 else 4
     return jax.shard_map(
         functools.partial(on_device, low, n_near),

time: 72.2 us -> 70.8 us (0.981); the launches traced: 71.1 us -> 70.6 us
  no operation moved by 1% of the time
where the time goes in v3:
time: 70.8 us; the launch traced here: 70.6 us
  Pallas kernels  68.7 us (97%)
  local copies, waits for them, and re-layouts  1.26 us (2%)
    pallas_call x1, Pallas kernels, on_device(): pl.pallas_call(functools.partial(kernel, dims), out_shape=jax.ShapeDtypeS...  68.7 us

profile of v3, /device:TPU:1, one launch (start us, length us, event | category | flops | bytes accessed | tf_op | source)
XLA Modules:
  0.0 70.6 jit_solution(8371938410126344320)
XLA Ops:
  0.7 68.7 %shard_map.82 = f32[6,1,128]{2,1,0:T(1,128)} custom-call(f32[3,8192]{1,0:T(4,128)} %pos_ref.1, f32[3,8192]{1,0:T(4,128)} %vel_ref.1, f32[3,8192]{1,0:T(4,128)} %acc_ref.1, f32[3,8192]{1,0:T(4,128)} %jerk_ref.1, f32[1,8192]{1,0:T(1,128)} %bitcast.6, f32[1,8192]{1,0:T(1,128)} %bitcast.7, s32[1,128]{1,0:T(1,128)} %bitcast.9, s32[1,1]{1,0:T(1,128)S(6)} %copy.11.count_ref), custom_call_target="tpu_custom_call" | custom-call | tf_op jit(solution)/shard_map/pallas_call | solution.py:480
  69.3 1.3 %copy.12 = f32[1,1,6,128]{3,1,2,0:T(1,128)} copy(f32[1,1,6,128]{3,1,2,0:T(1,128)} %bitcast.8) | data formatting | bytes 6144

commit v4 on v3

--- a/solution.py
+++ b/solution.py
@@ -130,11 +130,38 @@
         pl.semaphore_signal(barrier, 1, device_id={"blk": side}, device_id_type=MESH)
     pl.semaphore_signal(barrier, 1, device_id={"blk": other * low + column}, device_id_type=MESH)
 
-    for copy in fetch:
-        copy.wait()
+    fetch[6].wait()
     count = count_ref[0, 0]
     lane = lax.broadcasted_iota(jnp.int32, (1, LANES), 1)
     near[far] = jnp.where(lane < count, list_in[...], -1)
+
+    pl.semaphore_wait(barrier, (n_far - 1) + (n_near - 1) + low)
+
+    def a_copy(step, origin):
+        return pltpu.make_async_remote_copy(
+            src_ref=near.at[origin],
+            dst_ref=near.at[origin],
+            send_sem=a_send.at[step],
+            recv_sem=a_recv.at[step],
+            device_id={"group": far_peer(step) * n_near + close},
+            device_id_type=MESH,
+        )
+
+    def b_copy(step, origin):
+        return pltpu.make_async_remote_copy(
+            src_ref=near,
+            dst_ref=lists.at[origin],
+            send_sem=b_send.at[step],
+            recv_sem=b_recv.at[step],
+            device_id={"group": far * n_near + near_peer(step)},
+            device_id_type=MESH,
+        )
+
+    for step in range(1, n_far):
+        a_copy(step, far).start()
+
+    for copy in fetch[:6]:
+        copy.wait()
 
     width = min(1024, stars)
 
@@ -163,30 +190,6 @@
 
     lax.fori_loop(0, stars // width, predict, 0)
 
-    pl.semaphore_wait(barrier, (n_far - 1) + (n_near - 1) + low)
-
-    def a_copy(step, origin):
-        return pltpu.make_async_remote_copy(
-            src_ref=near.at[origin],
-            dst_ref=near.at[origin],
-            send_sem=a_send.at[step],
-            recv_sem=a_recv.at[step],
-            device_id={"group": far_peer(step) * n_near + close},
-            device_id_type=MESH,
-        )
-
-    def b_copy(step, origin):
-        return pltpu.make_async_remote_copy(
-            src_ref=near,
-            dst_ref=lists.at[origin],
-            send_sem=b_send.at[step],
-            recv_sem=b_recv.at[step],
-            device_id={"group": far * n_near + near_peer(step)},
-            device_id_type=MESH,
-        )
-
-    for step in range(1, n_far):
-        a_copy(step, far).start()
     for step in range(1, n_far):
         a_copy(step, lax.rem(far + n_far - step, n_far)).wait_recv()
     for step in range(1, n_near):
@@ -274,33 +277,7 @@
         peer = row * low + peer_at(place)
         r_copy(peer, b, peer).start()
 
-    span = min(2048, stars)
-    out_lane = lax.broadcasted_iota(jnp.int32, (ROWS, LANES), 1)
-
-    def pairs(index, carry):
-        line = peer_at(index)
-        away = (index >= early) & (index < early + low)
-        peer = jnp.where(away, other, row) * low + line
-
-        @pl.when(index == min(3, early))
-        def _():
-            r_copy(partner, partner, partner).wait_recv()
-            for step in range(1, low):
-                r_copy(row * low + side(step), partner, other * low + side(step)).start()
-
-        @pl.when((index > 0) & (index != early))
-        def _():
-            r_copy(peer, peer, peer).wait_recv()
-
-        @pl.when(index == n_blk - 1)
-        def _():
-            for step in range(1, low):
-                slot = other * low + side(low - step)
-                p_copy(b, slot, slot).wait_recv()
-            res[partner] = jnp.sum(part[pl.ds(other * low, low)], axis=0)
-            sum_copy.start()
-
-        own = rows[peer]
+    def chunk(own, height, span):
         own_pos, own_vel = own[0:3], own[3:6]
         inner = jnp.sum(own_pos * own_vel, axis=0, keepdims=True)
         mixed = jnp.concatenate([-own_vel, -own_pos, jnp.ones_like(inner), inner], axis=0)
@@ -309,8 +286,10 @@
         down = jnp.transpose(
             jnp.concatenate([big, big, mid, mid, big, small, own, fill], axis=0)
         )
-        mine_mixed = down[0:ROWS, 0:48].astype(jnp.bfloat16)
-        across = [jnp.broadcast_to(down[0:ROWS, 48 + c : 49 + c], (ROWS, LANES)) for c in range(3)]
+        mine_mixed = down[0:height, 0:48].astype(jnp.bfloat16)
+        across = [
+            jnp.broadcast_to(down[0:height, 48 + c : 49 + c], (height, LANES)) for c in range(3)
+        ]
 
         def advance(tile, carried):
             sums, sx, sy, sz = carried
@@ -321,7 +300,7 @@
             for part_at in range(0, span, LANES):
                 at = pl.ds(pl.multiple_of(base + part_at, LANES), LANES)
                 rx, ry, rz = (
-                    jnp.concatenate([wide[c, :, at]] * (ROWS // 8), axis=0) - across[c]
+                    jnp.concatenate([wide[c, :, at]] * (height // 8), axis=0) - across[c]
                     for c in range(3)
                 )
                 inverse = lax.rsqrt((rx * rx + ry * ry) + (rz * rz + soften))
@@ -337,48 +316,92 @@
             )
             return sums + product, sx, sy, sz
 
-        zero = jnp.zeros((ROWS, LANES), jnp.float32)
+        zero = jnp.zeros((height, LANES), jnp.float32)
         sums, sx, sy, sz = lax.fori_loop(
             0,
             stars // span,
             advance,
-            (jnp.zeros((ROWS, 32), jnp.float32), zero, zero, zero),
+            (jnp.zeros((height, 32), jnp.float32), zero, zero, zero),
             unroll=True,
         )
-        piece = jnp.concatenate([sums, jnp.zeros((ROWS, LANES - 32), jnp.float32)], axis=1)
+        out_lane = lax.broadcasted_iota(jnp.int32, (height, LANES), 1)
+        piece = jnp.concatenate([sums, jnp.zeros((height, LANES - 32), jnp.float32)], axis=1)
         for c, total in enumerate((sx, sy, sz)):
             piece = jnp.where(out_lane == 32 + c, jnp.sum(total, axis=1, keepdims=True), piece)
         up = jnp.transpose(
-            jnp.concatenate([piece, jnp.zeros((LANES - ROWS, LANES), jnp.float32)], axis=0)
+            jnp.concatenate([piece, jnp.zeros((LANES - height, LANES), jnp.float32)], axis=0)
         )
         moment = (up[0:8] + up[8:16]) + up[16:24]
         weighed = moment[6:7]
         accel = moment[0:3] - own_pos * weighed
         jerks = (moment[3:6] - own_vel * weighed) - 3.0 * up[32:35]
-        result = jnp.concatenate([accel, jerks, jnp.zeros((2, LANES), jnp.float32)], axis=0)
-
-        @pl.when(index == 0)
+        return jnp.concatenate([accel, jerks, jnp.zeros((2, LANES), jnp.float32)], axis=0)
+
+    def half_of(place):
+        return jnp.where((place >= early) & (place < early + low), other, row)
+
+    def collect(place):
+        peer = half_of(place) * low + peer_at(place)
+
+        @pl.when(place != early)
         def _():
-            part[b] = result
-
-        @pl.when(index == early)
+            r_copy(peer, peer, peer).wait_recv()
+
+        return rows[peer]
+
+    def deliver(place, result):
+        line, half = peer_at(place), half_of(place)
+        peer = half * low + line
+
+        @pl.when(place == early)
         def _():
             part[partner] = result
 
-        @pl.when((index > 0) & (index != early))
+        @pl.when(place != early)
         def _():
             res[peer] = result
-            p_copy(row * low + line, peer, jnp.where(away, other, row) * low + column).start()
-
+            p_copy(row * low + line, peer, half * low + column).start()
+
+    relay_at = min(3, early)
+
+    def pairs(index, carry):
+        first = 2 * index - 1
+
+        @pl.when(first == relay_at)
+        def _():
+            r_copy(partner, partner, partner).wait_recv()
+
+        def relay(step, carry):
+            r_copy(row * low + side(step), partner, other * low + side(step)).start()
+            return carry
+
+        lax.fori_loop(1, jnp.where(first == relay_at, low, 1), relay, 0)
+        own = collect(first) + pltpu.roll(collect(first + 1), ROWS, 1)
+        result = chunk(own, 2 * ROWS, min(1024, stars))
+        deliver(first, result)
+        deliver(first + 1, pltpu.roll(result, LANES - ROWS, 1))
         return carry
 
-    lax.fori_loop(0, n_blk, pairs, 0)
+    part[b] = chunk(rows[b], ROWS, min(2048, stars))
+    lax.fori_loop(1, n_blk // 2, pairs, 0)
+    for step in range(1, low):
+        slot = other * low + side(low - step)
+        p_copy(b, slot, slot).wait_recv()
+    res[partner] = jnp.sum(part[pl.ds(other * low, low)], axis=0)
+    sum_copy.start()
+    last = n_blk - 1
+    line = peer_at(last)
+    peer = row * low + line
+    r_copy(peer, peer, peer).wait_recv()
+    res[peer] = chunk(rows[peer], ROWS, min(2048, stars))
+    p_copy(peer, peer, b).start()
 
     for step in range(1, low):
         slot = row * low + side(low - step)
         p_copy(b, slot, slot).wait_recv()
     sum_copy.wait_recv()
     force = jnp.sum(part[pl.ds(row * low, low)], axis=0) + part[n_blk]
+    force = jnp.where(lane < ROWS, force, 0.0)
 
     per_tile = LANES // ROWS
     spread = force

time: 70.8 us -> 70.8 us (level)
  no operation moved by 1% of the time
where the time goes in v4:
time: 70.8 us; the launch traced here: 70.7 us
  Pallas kernels  68.7 us (97%)
  local copies, waits for them, and re-layouts  1.26 us (2%)
    pallas_call x1, Pallas kernels, on_device(): pl.pallas_call(functools.partial(kernel, dims), out_shape=jax.ShapeDtypeS...  68.7 us

profile of v4, /device:TPU:1, one launch (start us, length us, event | category | flops | bytes accessed | tf_op | source)
XLA Modules:
  0.0 70.7 jit_solution(1100418542265028944)
XLA Ops:
  0.7 68.7 %shard_map.82 = f32[6,1,128]{2,1,0:T(1,128)} custom-call(f32[3,8192]{1,0:T(4,128)} %pos_ref.1, f32[3,8192]{1,0:T(4,128)} %vel_ref.1, f32[3,8192]{1,0:T(4,128)} %acc_ref.1, f32[3,8192]{1,0:T(4,128)} %jerk_ref.1, f32[1,8192]{1,0:T(1,128)} %bitcast.6, f32[1,8192]{1,0:T(1,128)} %bitcast.7, s32[1,128]{1,0:T(1,128)} %bitcast.9, s32[1,1]{1,0:T(1,128)S(6)} %copy.11.count_ref), custom_call_target="tpu_custom_call" | custom-call | tf_op jit(solution)/shard_map/pallas_call | solution.py:503
  69.4 1.3 %copy.12 = f32[1,1,6,128]{3,1,2,0:T(1,128)} copy(f32[1,1,6,128]{3,1,2,0:T(1,128)} %bitcast.8) | data formatting | bytes 6144

commit v5 on v4

--- a/solution.py
+++ b/solution.py
@@ -382,7 +382,6 @@
         deliver(first + 1, pltpu.roll(result, LANES - ROWS, 1))
         return carry
 
-    part[b] = chunk(rows[b], ROWS, min(2048, stars))
     lax.fori_loop(1, n_blk // 2, pairs, 0)
     for step in range(1, low):
         slot = other * low + side(low - step)
@@ -395,6 +394,7 @@
     r_copy(peer, peer, peer).wait_recv()
     res[peer] = chunk(rows[peer], ROWS, min(2048, stars))
     p_copy(peer, peer, b).start()
+    part[b] = chunk(rows[b], ROWS, min(2048, stars))
 
     for step in range(1, low):
         slot = row * low + side(low - step)

time: 70.8 us -> 70.9 us (level)
  no operation moved by 1% of the time
where the time goes in v5:
time: 70.9 us; the launch traced here: 70.7 us
  Pallas kernels  68.8 us (97%)
  local copies, waits for them, and re-layouts  1.26 us (2%)
    pallas_call x1, Pallas kernels, on_device(): pl.pallas_call(functools.partial(kernel, dims), out_shape=jax.ShapeDtypeS...  68.8 us

profile of v5, /device:TPU:1, one launch (start us, length us, event | category | flops | bytes accessed | tf_op | source)
XLA Modules:
  0.0 70.7 jit_solution(3721106190713367280)
XLA Ops:
  0.7 68.8 %shard_map.82 = f32[6,1,128]{2,1,0:T(1,128)} custom-call(f32[3,8192]{1,0:T(4,128)} %pos_ref.1, f32[3,8192]{1,0:T(4,128)} %vel_ref.1, f32[3,8192]{1,0:T(4,128)} %acc_ref.1, f32[3,8192]{1,0:T(4,128)} %jerk_ref.1, f32[1,8192]{1,0:T(1,128)} %bitcast.6, f32[1,8192]{1,0:T(1,128)} %bitcast.7, s32[1,128]{1,0:T(1,128)} %bitcast.9, s32[1,1]{1,0:T(1,128)S(6)} %copy.11.count_ref), custom_call_target="tpu_custom_call" | custom-call | tf_op jit(solution)/shard_map/pallas_call | solution.py:503
  69.4 1.3 %copy.12 = f32[1,1,6,128]{3,1,2,0:T(1,128)} copy(f32[1,1,6,128]{3,1,2,0:T(1,128)} %bitcast.8) | data formatting | bytes 6144
